TPU v7x, 128 devices: a whole 4x4x4 slice. The times are simulated.
128 devices in a mesh: width: 4 (over z), row: 4 (over y), src: 8 (over x, core).
Axes of the slice: x: 4, y: 4, z: 4, core: 2. Of those that a mesh axis runs over, the one named last changes fastest.
Arguments:
- query_rows: bfloat16 [1024, 8192], P('row', 'width'), may hold values from -150 to 150
- key_rows: bfloat16 [1024, 1024], P('src', 'width'), may hold values from -7 to 7
- value_rows: bfloat16 [1024, 1024], P('src'), may hold values from -6 to 6
- out_proj: bfloat16 [8192, 8192], P(('row', 'src'), 'width'), may hold values from -0.0625 to 0.0625
Outputs:
- share: float32 [1024, 1024], P('row', ('src', 'width'))
All inputs are finite; a program needn't handle non-finite values.
Results may differ from a plain program's by a relative error of at most 0.0014.
Values may be sent and summed in bfloat16 or wider, within the bound.
A program may use at most 192 MiB of HBM per device.

v0:
```python
import math
import jax
import jax.numpy as jnp
from jax import lax
from jax.sharding import PartitionSpec as P

H = 64
KV = 8
HD = 128


def sent_to_all(shard, axis):
    copies = jnp.broadcast_to(shard, (lax.axis_size(axis), *shard.shape))
    return lax.all_to_all(copies, axis, split_axis=0, concat_axis=0, tiled=True)


def gathered_once(shard, axis):
    leaves = jax.tree.leaves(shard)
    sequence = sorted(range(len(leaves)), key=lambda k: -leaves[k].size)
    width = (1, *leaves[sequence[0]].shape)[-1]
    lines = [
        jnp.pad(leaves[k].reshape(-1), (0, -leaves[k].size % width)).reshape(-1, width)
        for k in sequence
    ]
    both, at, found = (sent_to_all(jnp.concatenate(lines), axis), 0, {})
    for k, line in zip(sequence, lines):
        slab = both[:, at : at + len(line)].reshape(len(both), -1)
        found[k] = slab[:, : leaves[k].size].reshape(-1, *leaves[k].shape)
        at += len(line)
    numbers = iter(range(len(leaves)))
    return jax.tree.map(lambda _: found[next(numbers)], shard)


def combined_pairwise(pieces, combine):
    while len(jax.tree.leaves(pieces)[0]) > 1:
        pieces = jax.vmap(combine)(
            *(jax.tree.map(lambda part: part[side::2], pieces) for side in (0, 1))
        )
    return jax.tree.map(lambda part: part[0], pieces)


def merged(shard, axis, combine):
    pieces = gathered_once(shard, axis)
    return combined_pairwise(pieces, combine)


def cut_along(shard, dim, size):
    dims = shard.shape
    parts = shard.reshape(*dims[:dim], size, dims[dim] // size, *dims[dim + 1 :])
    return jnp.moveaxis(parts, dim, 0)


def sum_at_owner(shard, axis, dim):
    size = lax.axis_size(axis)
    parts = lax.all_to_all(cut_along(shard, dim, size), axis, 0, 0, tiled=True)
    return jnp.sum(parts, axis=0)


def of_everyone(shard, axis):
    return sent_to_all(shard, axis).sum(axis=0)


def combine_stats(first, second):
    peak_one, mass_one = first
    peak_two, mass_two = second
    larger = jnp.maximum(peak_one, peak_two)
    return (larger, mass_one * jnp.exp(peak_one - larger) + mass_two * jnp.exp(peak_two - larger))


def body(query_rows, key_rows, value_rows, out_proj):
    here_row = lax.axis_index("row")
    here_src = lax.axis_index("src")
    row_count = query_rows.shape[0]
    col_count = key_rows.shape[0]
    group_size = H // KV
    row_pos = here_row * row_count + jnp.arange(row_count, dtype=jnp.int32)
    col_pos = here_src * col_count + jnp.arange(col_count, dtype=jnp.int32)
    local_heads = query_rows.shape[1] // HD
    local_kv = key_rows.shape[1] // HD
    queries = query_rows.reshape(row_count, local_kv, group_size, HD)
    key_heads = key_rows.reshape(col_count, local_kv, HD)
    scores = jnp.einsum("ikgd,jkd->kgij", queries, key_heads, preferred_element_type=jnp.float32)
    scores = scores.reshape(local_heads, row_count, col_count) / jnp.sqrt(jnp.float32(HD))
    causal = row_pos[:, None] >= col_pos[None, :]
    masked = jnp.where(causal, scores, jnp.float32(-1e30))
    row_peak = jnp.max(masked, axis=-1)
    row_mass = jnp.sum(jnp.where(causal, jnp.exp(masked - row_peak[..., None]), 0.0), axis=-1)
    row_peak, row_mass = merged((row_peak, row_mass), "src", combine_stats)
    weights = jnp.where(
        causal, jnp.exp(masked - row_peak[..., None]) / row_mass[..., None], 0.0
    ).astype(jnp.bfloat16)
    weights = lax.all_gather(weights, "width", axis=0, tiled=True)
    value_heads = value_rows.reshape(col_count, KV, HD)
    out_cols = out_proj.shape[1]
    proj_heads = out_proj.reshape(-1, HD, out_cols)
    portion = lax.all_gather(proj_heads, ("row", "src"), axis=0, tiled=True)
    head_count = portion.shape[0]
    head_ids = jnp.arange(head_count, dtype=jnp.int32)
    selector = (head_ids[:, None] // group_size == jnp.arange(KV, dtype=jnp.int32)[None, :]).astype(
        jnp.bfloat16
    )
    chosen = jnp.einsum(
        "hk,jkd->jhd", selector, value_heads, preferred_element_type=jnp.float32
    ).astype(jnp.bfloat16)
    images = jnp.einsum("jhd,hde->jhe", chosen, portion, preferred_element_type=jnp.float32).astype(
        jnp.bfloat16
    )
    row_block = math.gcd(row_count, 64)
    col_block = math.gcd(col_count, 32)
    col_steps = col_count // col_block
    turns = row_count // row_block * col_steps

    def tile(turn_index, running):
        row_start = turn_index // col_steps * row_block
        col_start = turn_index % col_steps * col_block
        row_slice = lax.dynamic_slice_in_dim(row_pos, row_start, row_block)
        col_slice = lax.dynamic_slice_in_dim(col_pos, col_start, col_block)

        def compute(unused):
            attend = lax.dynamic_slice(
                weights, (0, row_start, col_start), (H, row_block, col_block)
            )
            source_images = lax.dynamic_slice_in_dim(images, col_start, col_block, 0)
            contrib = jnp.einsum(
                "hij,jhe->ije", attend, source_images, preferred_element_type=jnp.float32
            )
            return jnp.sum(jnp.abs(contrib), axis=-1)

        def skipped(unused):
            return jnp.zeros((row_block, col_block), jnp.float32)

        result = lax.cond(jnp.max(row_slice) >= jnp.min(col_slice), compute, skipped, 0)
        return lax.dynamic_update_slice(running, result, (row_start, col_start))

    partial_value = lax.fori_loop(0, turns, tile, jnp.zeros((row_count, col_count), jnp.float32))
    summed = sum_at_owner(partial_value, "width", 1)
    totals = of_everyone(jnp.sum(summed, axis=1), ("width", "src"))
    position = (here_row * row_count + jnp.arange(row_count, dtype=jnp.int32) + 1).astype(
        jnp.float32
    )
    return position[:, None] * summed / totals[:, None]


def solution(mesh):
    placed = (P("row", "width"), P("src", "width"), P("src", None), P(("row", "src"), "width"))
    return jax.shard_map(
        body, mesh=mesh, in_specs=placed, out_specs=P("row", ("src", "width")), check_vma=False
    )
```

profile of v0, /device:TPU:25, one launch (start us, length us, event | category | flops | bytes accessed | tf_op | source)
XLA Modules:
  0.0 431.4 jit_solution(18067964968503341397)
XLA Ops:
  6.5 1.5 copy.36
  10.0 5.0 %all-to-all-start = ((f32[8,32,256]{2,1,0:T(8,128)}), f32[8,32,256]{2,1,0:T(8,128)S(1)}, u32[]{:S(2)}, u32[]{:S(2)}) async-start(f32[8,32,256]{2,1,0:T(8,128)} %broadcast_in_dim.44), calls=%async_computation | async-start | bytes 524288 | tf_op jit(solution)/shard_map/all_to_all | solution.py:14
  15.1 1.9 copy.27
  16.9 4.5 %all-to-all-done = f32[8,32,256]{2,1,0:T(8,128)S(1)} async-done(((f32[8,32,256]{2,1,0:T(8,128)}), f32[8,32,256]{2,1,0:T(8,128)S(1)}, u32[]{:S(2)}, u32[]{:S(2)}) %all-to-all-start) | async-done | bytes 262176 | tf_op jit(solution)/shard_map/all_to_all | solution.py:14
  21.6 4.1 select_convert_fusion
  27.2 47.7 %all-gather.5.cloned.1.call-done = bf16[64,256,128]{2,1,0:T(8,128)(2,1)} async-done(((bf16[16,256,128]{2,1,0:T(8,128)(2,1)}), bf16[64,256,128]{2,1,0:T(8,128)(2,1)}) %all-gather.5.cloned.1.call-update) | async-done | bytes 4194320 | tf_op jit(solution)/shard_map/all_gather | solution.py:92
  75.0 15.6 %copy.29 = bf16[64,256,128]{0,1,2:T(8,128)(2,1)} copy(bf16[64,256,128]{2,1,0:T(8,128)(2,1)} %all-gather.5.cloned.1.call-done) | data formatting | bytes 8388608 | tf_op jit(solution)/shard_map/while | solution.py:135
  90.6 100.2 %all-gather.3.cloned.1.call-done = bf16[64,128,2048]{2,1,0:T(8,128)(2,1)} async-done(((bf16[2,128,2048]{2,1,0:T(8,128)(2,1)}), bf16[64,128,2048]{2,1,0:T(8,128)(2,1)}) %all-gather.3.cloned.1.call-update) | async-done | bytes 33554448 | tf_op jit(solution)/shard_map/all_gather | solution.py:96
  190.8 24.2 %convert_bitcast_fusion = bf16[128,64,2048]{2,0,1:T(8,128)(2,1)} fusion(bf16[64,128,2048]{2,1,0:T(8,128)(2,1)} %all-gather.3.cloned.1.call-done, bf16[128,64,128]{2,1,0:T(8,128)(2,1)S(1)} %convert_bitcast_fusion.1), kind=kOutput, calls=%fused_computation.7 | convolution fusion | flops 4311744512 | bytes 69206016 | tf_op jit(solution)/shard_map/jhd,hde->jhe/dot_general | solution.py:105
  215.0 30.0 %copy.28 = bf16[128,64,2048]{2,1,0:T(8,128)(2,1)} copy(bf16[128,64,2048]{2,0,1:T(8,128)(2,1)} %convert_bitcast_fusion) | data formatting | bytes 67108864 | tf_op jit(solution)/shard_map/while | solution.py:135
  245.0 156.7 %while.15 = (s32[]{:T(128)}, f32[256,128]{0,1:T(8,128)S(1)}, s32[256]{0:T(256)S(1)}, s32[128]{0:T(128)S(1)}, bf16[128,64,2048]{2,1,0:T(8,128)(2,1)}, /*index=5*/...) while((s32[]{:T(128)}, f32[256,128]{0,1:T(8,128)S(1)}, ...), condition=%wide.region_8.9_spmd, body=%wide.region_2.8_spmd.sunk | while | flops 545257600 | bytes 8939898 | solution.py:135
  247.9 6.0 %conditional.2 = (f32[64,32]{0,1:T(8,128)S(1)}) conditional(s32[]{:T(128)} %convert_element_type.44, () %tuple.54, (s32[]{:T(128)}, bf16[128,64,2048]{2,1,0:T(8,128)(2,1)}, s32[]{:T(128)}, bf16[64,256,128]{0,1,2:T(8,128)(2,1)}) %tuple.55), branch_computations={%region_5.5_spmd, %region_6.7_spmd} | conditional | flops 545257472 | bytes 8922700 | solution.py:132
  247.9 6.0 %abs_reduce_fusion = f32[32,64]{1,0:T(8,128)S(1)} fusion(bf16[128,64,2048]{2,1,0:T(8,128)(2,1)} %get-tuple-element.172, s32[]{:T(128)S(6)} %select_n.76, bf16[64,256,128]{0,1,2:T(8,128)(2,1)} %get-tuple-element.174, s32[]{:T(128)S(6)} %select_n.77), kind=kOutput, calls=%fused_computation | convolution fusion | flops 545257472 | bytes 8922624 | tf_op jit(solution)/shard_map/while/body/eval_jaxpr/cond/branch_1_fun/hij,jhe->ije/dot_general | solution.py:124
  257.7 6.0 %conditional.2 = (f32[64,32]{0,1:T(8,128)S(1)}) conditional(s32[]{:T(128)} %convert_element_type.44, () %tuple.54, (s32[]{:T(128)}, bf16[128,64,2048]{2,1,0:T(8,128)(2,1)}, s32[]{:T(128)}, bf16[64,256,128]{0,1,2:T(8,128)(2,1)}) %tuple.55), branch_computations={%region_5.5_spmd, %region_6.7_spmd} | conditional | flops 545257472 | bytes 8922700 | solution.py:132
  257.7 6.0 %abs_reduce_fusion = f32[32,64]{1,0:T(8,128)S(1)} fusion(bf16[128,64,2048]{2,1,0:T(8,128)(2,1)} %get-tuple-element.172, s32[]{:T(128)S(6)} %select_n.76, bf16[64,256,128]{0,1,2:T(8,128)(2,1)} %get-tuple-element.174, s32[]{:T(128)S(6)} %select_n.77), kind=kOutput, calls=%fused_computation | convolution fusion | flops 545257472 | bytes 8922624 | tf_op jit(solution)/shard_map/while/body/eval_jaxpr/cond/branch_1_fun/hij,jhe->ije/dot_general | solution.py:124
  267.5 6.0 %conditional.2 = (f32[64,32]{0,1:T(8,128)S(1)}) conditional(s32[]{:T(128)} %convert_element_type.44, () %tuple.54, (s32[]{:T(128)}, bf16[128,64,2048]{2,1,0:T(8,128)(2,1)}, s32[]{:T(128)}, bf16[64,256,128]{0,1,2:T(8,128)(2,1)}) %tuple.55), branch_computations={%region_5.5_spmd, %region_6.7_spmd} | conditional | flops 545257472 | bytes 8922700 | solution.py:132
  267.5 6.0 %abs_reduce_fusion = f32[32,64]{1,0:T(8,128)S(1)} fusion(bf16[128,64,2048]{2,1,0:T(8,128)(2,1)} %get-tuple-element.172, s32[]{:T(128)S(6)} %select_n.76, bf16[64,256,128]{0,1,2:T(8,128)(2,1)} %get-tuple-element.174, s32[]{:T(128)S(6)} %select_n.77), kind=kOutput, calls=%fused_computation | convolution fusion | flops 545257472 | bytes 8922624 | tf_op jit(solution)/shard_map/while/body/eval_jaxpr/cond/branch_1_fun/hij,jhe->ije/dot_general | solution.py:124
  277.3 6.0 %conditional.2 = (f32[64,32]{0,1:T(8,128)S(1)}) conditional(s32[]{:T(128)} %convert_element_type.44, () %tuple.54, (s32[]{:T(128)}, bf16[128,64,2048]{2,1,0:T(8,128)(2,1)}, s32[]{:T(128)}, bf16[64,256,128]{0,1,2:T(8,128)(2,1)}) %tuple.55), branch_computations={%region_5.5_spmd, %region_6.7_spmd} | conditional | flops 545257472 | bytes 8922700 | solution.py:132
  277.3 6.0 %abs_reduce_fusion = f32[32,64]{1,0:T(8,128)S(1)} fusion(bf16[128,64,2048]{2,1,0:T(8,128)(2,1)} %get-tuple-element.172, s32[]{:T(128)S(6)} %select_n.76, bf16[64,256,128]{0,1,2:T(8,128)(2,1)} %get-tuple-element.174, s32[]{:T(128)S(6)} %select_n.77), kind=kOutput, calls=%fused_computation | convolution fusion | flops 545257472 | bytes 8922624 | tf_op jit(solution)/shard_map/while/body/eval_jaxpr/cond/branch_1_fun/hij,jhe->ije/dot_general | solution.py:124
  286.9 6.0 %conditional.2 = (f32[64,32]{0,1:T(8,128)S(1)}) conditional(s32[]{:T(128)} %convert_element_type.44, () %tuple.54, (s32[]{:T(128)}, bf16[128,64,2048]{2,1,0:T(8,128)(2,1)}, s32[]{:T(128)}, bf16[64,256,128]{0,1,2:T(8,128)(2,1)}) %tuple.55), branch_computations={%region_5.5_spmd, %region_6.7_spmd} | conditional | flops 545257472 | bytes 8922700 | solution.py:132
  286.9 6.0 %abs_reduce_fusion = f32[32,64]{1,0:T(8,128)S(1)} fusion(bf16[128,64,2048]{2,1,0:T(8,128)(2,1)} %get-tuple-element.172, s32[]{:T(128)S(6)} %select_n.76, bf16[64,256,128]{0,1,2:T(8,128)(2,1)} %get-tuple-element.174, s32[]{:T(128)S(6)} %select_n.77), kind=kOutput, calls=%fused_computation | convolution fusion | flops 545257472 | bytes 8922624 | tf_op jit(solution)/shard_map/while/body/eval_jaxpr/cond/branch_1_fun/hij,jhe->ije/dot_general | solution.py:124
  292.9 1.1 dynamic_update_slice.11
  297.0 6.0 %conditional.2 = (f32[64,32]{0,1:T(8,128)S(1)}) conditional(s32[]{:T(128)} %convert_element_type.44, () %tuple.54, (s32[]{:T(128)}, bf16[128,64,2048]{2,1,0:T(8,128)(2,1)}, s32[]{:T(128)}, bf16[64,256,128]{0,1,2:T(8,128)(2,1)}) %tuple.55), branch_computations={%region_5.5_spmd, %region_6.7_spmd} | conditional | flops 545257472 | bytes 8922700 | solution.py:132
  297.0 6.0 %abs_reduce_fusion = f32[32,64]{1,0:T(8,128)S(1)} fusion(bf16[128,64,2048]{2,1,0:T(8,128)(2,1)} %get-tuple-element.172, s32[]{:T(128)S(6)} %select_n.76, bf16[64,256,128]{0,1,2:T(8,128)(2,1)} %get-tuple-element.174, s32[]{:T(128)S(6)} %select_n.77), kind=kOutput, calls=%fused_computation | convolution fusion | flops 545257472 | bytes 8922624 | tf_op jit(solution)/shard_map/while/body/eval_jaxpr/cond/branch_1_fun/hij,jhe->ije/dot_general | solution.py:124
  303.0 1.1 dynamic_update_slice.11
  307.0 6.0 %conditional.2 = (f32[64,32]{0,1:T(8,128)S(1)}) conditional(s32[]{:T(128)} %convert_element_type.44, () %tuple.54, (s32[]{:T(128)}, bf16[128,64,2048]{2,1,0:T(8,128)(2,1)}, s32[]{:T(128)}, bf16[64,256,128]{0,1,2:T(8,128)(2,1)}) %tuple.55), branch_computations={%region_5.5_spmd, %region_6.7_spmd} | conditional | flops 545257472 | bytes 8922700 | solution.py:132
  307.1 6.0 %abs_reduce_fusion = f32[32,64]{1,0:T(8,128)S(1)} fusion(bf16[128,64,2048]{2,1,0:T(8,128)(2,1)} %get-tuple-element.172, s32[]{:T(128)S(6)} %select_n.76, bf16[64,256,128]{0,1,2:T(8,128)(2,1)} %get-tuple-element.174, s32[]{:T(128)S(6)} %select_n.77), kind=kOutput, calls=%fused_computation | convolution fusion | flops 545257472 | bytes 8922624 | tf_op jit(solution)/shard_map/while/body/eval_jaxpr/cond/branch_1_fun/hij,jhe->ije/dot_general | solution.py:124
  317.1 6.0 %conditional.2 = (f32[64,32]{0,1:T(8,128)S(1)}) conditional(s32[]{:T(128)} %convert_element_type.44, () %tuple.54, (s32[]{:T(128)}, bf16[128,64,2048]{2,1,0:T(8,128)(2,1)}, s32[]{:T(128)}, bf16[64,256,128]{0,1,2:T(8,128)(2,1)}) %tuple.55), branch_computations={%region_5.5_spmd, %region_6.7_spmd} | conditional | flops 545257472 | bytes 8922700 | solution.py:132
  317.1 6.0 %abs_reduce_fusion = f32[32,64]{1,0:T(8,128)S(1)} fusion(bf16[128,64,2048]{2,1,0:T(8,128)(2,1)} %get-tuple-element.172, s32[]{:T(128)S(6)} %select_n.76, bf16[64,256,128]{0,1,2:T(8,128)(2,1)} %get-tuple-element.174, s32[]{:T(128)S(6)} %select_n.77), kind=kOutput, calls=%fused_computation | convolution fusion | flops 545257472 | bytes 8922624 | tf_op jit(solution)/shard_map/while/body/eval_jaxpr/cond/branch_1_fun/hij,jhe->ije/dot_general | solution.py:124
  327.0 6.0 %conditional.2 = (f32[64,32]{0,1:T(8,128)S(1)}) conditional(s32[]{:T(128)} %convert_element_type.44, () %tuple.54, (s32[]{:T(128)}, bf16[128,64,2048]{2,1,0:T(8,128)(2,1)}, s32[]{:T(128)}, bf16[64,256,128]{0,1,2:T(8,128)(2,1)}) %tuple.55), branch_computations={%region_5.5_spmd, %region_6.7_spmd} | conditional | flops 545257472 | bytes 8922700 | solution.py:132
  327.0 6.0 %abs_reduce_fusion = f32[32,64]{1,0:T(8,128)S(1)} fusion(bf16[128,64,2048]{2,1,0:T(8,128)(2,1)} %get-tuple-element.172, s32[]{:T(128)S(6)} %select_n.76, bf16[64,256,128]{0,1,2:T(8,128)(2,1)} %get-tuple-element.174, s32[]{:T(128)S(6)} %select_n.77), kind=kOutput, calls=%fused_computation | convolution fusion | flops 545257472 | bytes 8922624 | tf_op jit(solution)/shard_map/while/body/eval_jaxpr/cond/branch_1_fun/hij,jhe->ije/dot_general | solution.py:124
  336.6 6.0 %conditional.2 = (f32[64,32]{0,1:T(8,128)S(1)}) conditional(s32[]{:T(128)} %convert_element_type.44, () %tuple.54, (s32[]{:T(128)}, bf16[128,64,2048]{2,1,0:T(8,128)(2,1)}, s32[]{:T(128)}, bf16[64,256,128]{0,1,2:T(8,128)(2,1)}) %tuple.55), branch_computations={%region_5.5_spmd, %region_6.7_spmd} | conditional | flops 545257472 | bytes 8922700 | solution.py:132
  336.6 6.0 %abs_reduce_fusion = f32[32,64]{1,0:T(8,128)S(1)} fusion(bf16[128,64,2048]{2,1,0:T(8,128)(2,1)} %get-tuple-element.172, s32[]{:T(128)S(6)} %select_n.76, bf16[64,256,128]{0,1,2:T(8,128)(2,1)} %get-tuple-element.174, s32[]{:T(128)S(6)} %select_n.77), kind=kOutput, calls=%fused_computation | convolution fusion | flops 545257472 | bytes 8922624 | tf_op jit(solution)/shard_map/while/body/eval_jaxpr/cond/branch_1_fun/hij,jhe->ije/dot_general | solution.py:124
  346.2 6.0 %conditional.2 = (f32[64,32]{0,1:T(8,128)S(1)}) conditional(s32[]{:T(128)} %convert_element_type.44, () %tuple.54, (s32[]{:T(128)}, bf16[128,64,2048]{2,1,0:T(8,128)(2,1)}, s32[]{:T(128)}, bf16[64,256,128]{0,1,2:T(8,128)(2,1)}) %tuple.55), branch_computations={%region_5.5_spmd, %region_6.7_spmd} | conditional | flops 545257472 | bytes 8922700 | solution.py:132
  346.2 6.0 %abs_reduce_fusion = f32[32,64]{1,0:T(8,128)S(1)} fusion(bf16[128,64,2048]{2,1,0:T(8,128)(2,1)} %get-tuple-element.172, s32[]{:T(128)S(6)} %select_n.76, bf16[64,256,128]{0,1,2:T(8,128)(2,1)} %get-tuple-element.174, s32[]{:T(128)S(6)} %select_n.77), kind=kOutput, calls=%fused_computation | convolution fusion | flops 545257472 | bytes 8922624 | tf_op jit(solution)/shard_map/while/body/eval_jaxpr/cond/branch_1_fun/hij,jhe->ije/dot_general | solution.py:124
  355.8 6.0 %conditional.2 = (f32[64,32]{0,1:T(8,128)S(1)}) conditional(s32[]{:T(128)} %convert_element_type.44, () %tuple.54, (s32[]{:T(128)}, bf16[128,64,2048]{2,1,0:T(8,128)(2,1)}, s32[]{:T(128)}, bf16[64,256,128]{0,1,2:T(8,128)(2,1)}) %tuple.55), branch_computations={%region_5.5_spmd, %region_6.7_spmd} | conditional | flops 545257472 | bytes 8922700 | solution.py:132
  355.8 6.0 %abs_reduce_fusion = f32[32,64]{1,0:T(8,128)S(1)} fusion(bf16[128,64,2048]{2,1,0:T(8,128)(2,1)} %get-tuple-element.172, s32[]{:T(128)S(6)} %select_n.76, bf16[64,256,128]{0,1,2:T(8,128)(2,1)} %get-tuple-element.174, s32[]{:T(128)S(6)} %select_n.77), kind=kOutput, calls=%fused_computation | convolution fusion | flops 545257472 | bytes 8922624 | tf_op jit(solution)/shard_map/while/body/eval_jaxpr/cond/branch_1_fun/hij,jhe->ije/dot_general | solution.py:124
  365.2 6.0 %conditional.2 = (f32[64,32]{0,1:T(8,128)S(1)}) conditional(s32[]{:T(128)} %convert_element_type.44, () %tuple.54, (s32[]{:T(128)}, bf16[128,64,2048]{2,1,0:T(8,128)(2,1)}, s32[]{:T(128)}, bf16[64,256,128]{0,1,2:T(8,128)(2,1)}) %tuple.55), branch_computations={%region_5.5_spmd, %region_6.7_spmd} | conditional | flops 545257472 | bytes 8922700 | solution.py:132
  365.3 6.0 %abs_reduce_fusion = f32[32,64]{1,0:T(8,128)S(1)} fusion(bf16[128,64,2048]{2,1,0:T(8,128)(2,1)} %get-tuple-element.172, s32[]{:T(128)S(6)} %select_n.76, bf16[64,256,128]{0,1,2:T(8,128)(2,1)} %get-tuple-element.174, s32[]{:T(128)S(6)} %select_n.77), kind=kOutput, calls=%fused_computation | convolution fusion | flops 545257472 | bytes 8922624 | tf_op jit(solution)/shard_map/while/body/eval_jaxpr/cond/branch_1_fun/hij,jhe->ije/dot_general | solution.py:124
  375.1 6.0 %conditional.2 = (f32[64,32]{0,1:T(8,128)S(1)}) conditional(s32[]{:T(128)} %convert_element_type.44, () %tuple.54, (s32[]{:T(128)}, bf16[128,64,2048]{2,1,0:T(8,128)(2,1)}, s32[]{:T(128)}, bf16[64,256,128]{0,1,2:T(8,128)(2,1)}) %tuple.55), branch_computations={%region_5.5_spmd, %region_6.7_spmd} | conditional | flops 545257472 | bytes 8922700 | solution.py:132
  375.1 6.0 %abs_reduce_fusion = f32[32,64]{1,0:T(8,128)S(1)} fusion(bf16[128,64,2048]{2,1,0:T(8,128)(2,1)} %get-tuple-element.172, s32[]{:T(128)S(6)} %select_n.76, bf16[64,256,128]{0,1,2:T(8,128)(2,1)} %get-tuple-element.174, s32[]{:T(128)S(6)} %select_n.77), kind=kOutput, calls=%fused_computation | convolution fusion | flops 545257472 | bytes 8922624 | tf_op jit(solution)/shard_map/while/body/eval_jaxpr/cond/branch_1_fun/hij,jhe->ije/dot_general | solution.py:124
  384.9 6.0 %conditional.2 = (f32[64,32]{0,1:T(8,128)S(1)}) conditional(s32[]{:T(128)} %convert_element_type.44, () %tuple.54, (s32[]{:T(128)}, bf16[128,64,2048]{2,1,0:T(8,128)(2,1)}, s32[]{:T(128)}, bf16[64,256,128]{0,1,2:T(8,128)(2,1)}) %tuple.55), branch_computations={%region_5.5_spmd, %region_6.7_spmd} | conditional | flops 545257472 | bytes 8922700 | solution.py:132
  385.0 6.0 %abs_reduce_fusion = f32[32,64]{1,0:T(8,128)S(1)} fusion(bf16[128,64,2048]{2,1,0:T(8,128)(2,1)} %get-tuple-element.172, s32[]{:T(128)S(6)} %select_n.76, bf16[64,256,128]{0,1,2:T(8,128)(2,1)} %get-tuple-element.174, s32[]{:T(128)S(6)} %select_n.77), kind=kOutput, calls=%fused_computation | convolution fusion | flops 545257472 | bytes 8922624 | tf_op jit(solution)/shard_map/while/body/eval_jaxpr/cond/branch_1_fun/hij,jhe->ije/dot_general | solution.py:124
  394.8 6.0 %conditional.2 = (f32[64,32]{0,1:T(8,128)S(1)}) conditional(s32[]{:T(128)} %convert_element_type.44, () %tuple.54, (s32[]{:T(128)}, bf16[128,64,2048]{2,1,0:T(8,128)(2,1)}, s32[]{:T(128)}, bf16[64,256,128]{0,1,2:T(8,128)(2,1)}) %tuple.55), branch_computations={%region_5.5_spmd, %region_6.7_spmd} | conditional | flops 545257472 | bytes 8922700 | solution.py:132
  394.8 6.0 %abs_reduce_fusion = f32[32,64]{1,0:T(8,128)S(1)} fusion(bf16[128,64,2048]{2,1,0:T(8,128)(2,1)} %get-tuple-element.172, s32[]{:T(128)S(6)} %select_n.76, bf16[64,256,128]{0,1,2:T(8,128)(2,1)} %get-tuple-element.174, s32[]{:T(128)S(6)} %select_n.77), kind=kOutput, calls=%fused_computation | convolution fusion | flops 545257472 | bytes 8922624 | tf_op jit(solution)/shard_map/while/body/eval_jaxpr/cond/branch_1_fun/hij,jhe->ije/dot_general | solution.py:124
  401.7 8.7 %all_to_all.16 = f32[4,256,32]{1,2,0:T(8,128)S(1)} all-to-all(f32[4,256,32]{1,2,0:T(8,128)S(1)} %bitcast.40), channel_id=1, replica_groups=mesh['width'=4,'row'=4,'src'=8] {'width'}, dimensions={0} | all-to-all | bytes 262144 | tf_op jit(solution)/shard_map/all_to_all | solution.py:55
  411.1 5.6 %all-to-all-start.2 = ((f32[32,1,256]{2,1,0:T(1,128)}), f32[32,1,256]{2,1,0:T(1,128)S(1)}, u32[]{:S(2)}, u32[]{:S(2)}) async-start(f32[32,1,256]{2,1,0:T(1,128)} %broadcast_in_dim.46), calls=%async_computation.2 | async-start | bytes 65536 | tf_op jit(solution)/shard_map/all_to_all | solution.py:14
  416.6 7.2 %all-to-all-done.2 = f32[32,1,256]{2,1,0:T(1,128)S(1)} async-done(((f32[32,1,256]{2,1,0:T(1,128)}), f32[32,1,256]{2,1,0:T(1,128)S(1)}, u32[]{:S(2)}, u32[]{:S(2)}) %all-to-all-start.2) | async-done | bytes 32800 | tf_op jit(solution)/shard_map/all_to_all | solution.py:14
  (76 shorter events, 41.2 us)
Async XLA Ops:
  6.5 1.5 copy-start.1
  10.0 11.5 %all-to-all-start = ((f32[8,32,256]{2,1,0:T(8,128)}), f32[8,32,256]{2,1,0:T(8,128)S(1)}, u32[]{:S(2)}, u32[]{:S(2)}) async-start(f32[8,32,256]{2,1,0:T(8,128)} %broadcast_in_dim.44), calls=%async_computation | async-start | bytes 524288 | tf_op jit(solution)/shard_map/all_to_all | solution.py:14
  14.9 60.0 %all-gather.5.cloned.1.call-start = ((), (), s32[]{:S(2)}) async-start(), calls=%async_computation.4 | async-start | bytes 5242880 | tf_op jit(solution)/shard_map/all_gather | solution.py:92
  21.6 4.9 %copy-start = (bf16[128,1024]{1,0:T(8,128)(2,1)S(1)}, bf16[128,1024]{1,0:T(8,128)(2,1)}, u32[]{:S(2)}) copy-start(bf16[128,1024]{1,0:T(8,128)(2,1)} %param.10) | copy-start | bytes 786436
  25.7 165.1 %all-gather.3.cloned.1.call-start = ((), (), s32[]{:S(2)}) async-start(), calls=%async_computation.3 | async-start | bytes 34603008 | tf_op jit(solution)/shard_map/all_gather | solution.py:96
  411.1 12.8 %all-to-all-start.2 = ((f32[32,1,256]{2,1,0:T(1,128)}), f32[32,1,256]{2,1,0:T(1,128)S(1)}, u32[]{:S(2)}, u32[]{:S(2)}) async-start(f32[32,1,256]{2,1,0:T(1,128)} %broadcast_in_dim.46), calls=%async_computation.2 | async-start | bytes 65536 | tf_op jit(solution)/shard_map/all_to_all | solution.py:14
Sparse Core Ops, SparseCore 0:
  25.8 49.1 all-gather.4
  77.2 113.4 all-gather.2
where the time goes:
time: 432 us; the launch traced here: 431 us
  waiting for transfers between devices  160 us (37%)
  matrix products  122 us (28%)
  local copies, waits for them, and re-layouts  64.2 us (15%)
  other arithmetic  30.2 us (7%)
  loops' own time  22.2 us (5%)
  between operations  13.6 us (3%)
  starting transfers between devices  10.8 us (2%)
  blocking collectives  8.75 us (2%)
    all_gather x1, waiting for transfers between devices, body(): portion = lax.all_gather(proj_heads, ('row', 'src'), axis=0, tiled=True)  100 us
    dot_general x16, matrix products, compute(): jnp.einsum('hij,jhe->ije', attend, source_images, preferred_element_type=...  96.1 us
    all_gather x1, waiting for transfers between devices, body(): weights = lax.all_gather(weights, 'width', axis=0, tiled=True)  47.7 us
    while x2, local copies, waits for them, and re-layouts, body(): lax.fori_loop(0, turns, tile, jnp.zeros((row_count, col_count), jnp.float...  45.6 us
    dot_general x1, matrix products, body(): jnp.einsum('jhd,hde->jhe', chosen, portion, preferred_element_type=jnp.fl...  24.2 us
    another operation x1, loops' own time, body(): lax.fori_loop(0, turns, tile, jnp.zeros((row_count, col_count), jnp.float...  21.8 us
    dynamic_update_slice x16, local copies, waits for them, and re-layouts, tile(): return lax.dynamic_update_slice(running, result, (row_start, col_start))  13.7 us
    reduce_max x16, other arithmetic, tile(): jnp.max(row_slice) >= jnp.min(col_slice)  12.5 us
  transfers between devices with their start and end apart: 4, of which 4 were waited for; matrix products, arithmetic and copies ran while one was open for 4% of the time, Pallas kernels for 0%

commit v1 on v0

--- a/solution.py
+++ b/solution.py
@@ -89,7 +89,16 @@
     weights = jnp.where(
         causal, jnp.exp(masked - row_peak[..., None]) / row_mass[..., None], 0.0
     ).astype(jnp.bfloat16)
-    weights = lax.all_gather(weights, "width", axis=0, tiled=True)
+    ways = lax.axis_size("width")
+    up = [(d, (d + 1) % ways) for d in range(ways)]
+    down = [(d, (d - 1) % ways) for d in range(ways)]
+    earlier, later = ([weights], [weights])
+    for __2 in range(ways // 2):
+        earlier.append(lax.ppermute(earlier[-1], "width", up))
+    for __2 in range((ways - 1) // 2):
+        later.append(lax.ppermute(later[-1], "width", down))
+    line_2 = jnp.concatenate([*earlier[::-1], *later[1:]], axis=0)
+    weights = jnp.roll(line_2, (lax.axis_index("width") - ways // 2) * weights.shape[0], axis=0)
     value_heads = value_rows.reshape(col_count, KV, HD)
     out_cols = out_proj.shape[1]
     proj_heads = out_proj.reshape(-1, HD, out_cols)

time: 432 us -> 367 us (0.85)
  waiting for transfers between devices: 160 us -> 78.2 us
  local copies, waits for them, and re-layouts: 64.2 us -> 73.7 us
    all_gather x1, waiting for transfers between devices: 100 us -> 22.5 us  [body(): portion = lax.all_gather(proj_heads, ('row', 'src'), axis=0, tiled=True)]
    all_gather x1 -> x0, waiting for transfers between devices: 47.7 us -> none  [body(): weights = lax.all_gather(weights, 'width', axis=0, tiled=True)]
    ppermute x0 -> x3, waiting for transfers between devices: none -> 43.3 us  [the longest x2 43.3 us: body(): earlier.append(lax.ppermute(earlier[-1], 'width', up))]
    unnamed x6 -> x13, local copies, waits for them, and re-layouts: 1.53 us -> 6.94 us
  transfers between devices with their start and end apart: 4 -> 6, of which waited for: 4 -> 5; matrix products, arithmetic and copies ran while one was open for 4% -> 10% of each run, Pallas kernels for 0% -> 0%
where the time goes in v1:
time: 367 us; the launch traced here: 366 us
  matrix products  123 us (34%)
  waiting for transfers between devices  78.2 us (21%)
  local copies, waits for them, and re-layouts  73.7 us (20%)
  other arithmetic  31.5 us (9%)
  loops' own time  22.2 us (6%)
  starting transfers between devices  14.8 us (4%)
  between operations  13.6 us (4%)
  blocking collectives  8.8 us (2%)
    dot_general x16, matrix products, compute(): jnp.einsum('hij,jhe->ije', attend, source_images, preferred_element_type=...  96.1 us
    while x2, local copies, waits for them, and re-layouts, body(): lax.fori_loop(0, turns, tile, jnp.zeros((row_count, col_count), jnp.float...  45.7 us
    ppermute x2, waiting for transfers between devices, body(): earlier.append(lax.ppermute(earlier[-1], 'width', up))  43.3 us
    dot_general x1, matrix products, body(): jnp.einsum('jhd,hde->jhe', chosen, portion, preferred_element_type=jnp.fl...  24.2 us
    all_gather x1, waiting for transfers between devices, body(): portion = lax.all_gather(proj_heads, ('row', 'src'), axis=0, tiled=True)  22.5 us
    another operation x1, loops' own time, body(): lax.fori_loop(0, turns, tile, jnp.zeros((row_count, col_count), jnp.float...  21.8 us
    dynamic_update_slice x16, local copies, waits for them, and re-layouts, tile(): return lax.dynamic_update_slice(running, result, (row_start, col_start))  13.7 us
    reduce_max x16, other arithmetic, tile(): jnp.max(row_slice) >= jnp.min(col_slice)  12.5 us
  transfers between devices with their start and end apart: 6, of which 5 were waited for; matrix products, arithmetic and copies ran while one was open for 10% of the time, Pallas kernels for 0%

profile of v1, /device:TPU:25, one launch (start us, length us, event | category | flops | bytes accessed | tf_op | source)
XLA Modules:
  0.0 365.7 jit_solution(11068839865914366792)
XLA Ops:
  10.9 5.0 %all-to-all-start = ((f32[8,32,256]{2,1,0:T(8,128)}), f32[8,32,256]{2,1,0:T(8,128)S(1)}, u32[]{:S(2)}, u32[]{:S(2)}) async-start(f32[8,32,256]{2,1,0:T(8,128)} %broadcast_in_dim.44), calls=%async_computation | async-start | bytes 524288 | tf_op jit(solution)/shard_map/all_to_all | solution.py:14
  17.9 4.4 %all-to-all-done = f32[8,32,256]{2,1,0:T(8,128)S(1)} async-done(((f32[8,32,256]{2,1,0:T(8,128)}), f32[8,32,256]{2,1,0:T(8,128)S(1)}, u32[]{:S(2)}, u32[]{:S(2)}) %all-to-all-start) | async-done | bytes 262176 | tf_op jit(solution)/shard_map/all_to_all | solution.py:14
  22.5 2.1 select_convert_fusion
  26.2 24.8 %collective-permute-done = bf16[16,256,128]{2,1,0:T(8,128)(2,1)S(1)} collective-permute-done((bf16[16,256,128]{2,1,0:T(8,128)(2,1)}, bf16[16,256,128]{2,1,0:T(8,128)(2,1)S(1)}, u32[]{:S(2)}, u32[]{:S(2)}) %collective-permute-start) | collective-permute-done | bytes 1048608 | tf_op jit(solution)/shard_map/ppermute | solution.py:97
  51.0 2.7 collective-permute-start.2
  54.7 2.0 convert_bitcast_fusion.1
  56.8 18.5 %collective-permute-done.1 = bf16[16,256,128]{2,1,0:T(8,128)(2,1)} collective-permute-done((bf16[16,256,128]{2,1,0:T(8,128)(2,1)S(1)}, bf16[16,256,128]{2,1,0:T(8,128)(2,1)}, u32[]{:S(2)}, u32[]{:S(2)}) %collective-permute-start.1) | collective-permute-done | bytes 1048608 | tf_op jit(solution)/shard_map/ppermute | solution.py:97
  84.5 2.3 constant_dynamic-slice_fusion
  86.9 15.8 %copy.29 = bf16[64,256,128]{0,1,2:T(8,128)(2,1)} copy(bf16[64,256,128]{2,1,0:T(8,128)(2,1)} %constant_dynamic-slice_fusion) | data formatting | bytes 8388608 | tf_op jit(solution)/shard_map/while | solution.py:144
  102.6 22.5 %all-gather.2.cloned.1.call-done = bf16[64,128,2048]{2,1,0:T(8,128)(2,1)} async-done(((bf16[2,128,2048]{2,1,0:T(8,128)(2,1)}), bf16[64,128,2048]{2,1,0:T(8,128)(2,1)}) %all-gather.2.cloned.1.call-update) | async-done | bytes 33554448 | tf_op jit(solution)/shard_map/all_gather | solution.py:105
  125.1 24.2 %convert_bitcast_fusion = bf16[128,64,2048]{2,0,1:T(8,128)(2,1)} fusion(bf16[64,128,2048]{2,1,0:T(8,128)(2,1)} %all-gather.2.cloned.1.call-done, bf16[128,64,128]{2,1,0:T(8,128)(2,1)S(1)} %copy-done.1), kind=kOutput, calls=%fused_computation.7 | convolution fusion | flops 4311744512 | bytes 69206016 | tf_op jit(solution)/shard_map/jhd,hde->jhe/dot_general | solution.py:114
  149.3 30.0 %copy.28 = bf16[128,64,2048]{2,1,0:T(8,128)(2,1)} copy(bf16[128,64,2048]{2,0,1:T(8,128)(2,1)} %convert_bitcast_fusion) | data formatting | bytes 67108864 | tf_op jit(solution)/shard_map/while | solution.py:144
  179.3 156.7 %while.15 = (s32[]{:T(128)}, f32[256,128]{0,1:T(8,128)S(1)}, s32[256]{0:T(256)S(1)}, s32[128]{0:T(128)S(1)}, bf16[128,64,2048]{2,1,0:T(8,128)(2,1)}, /*index=5*/...) while((s32[]{:T(128)}, f32[256,128]{0,1:T(8,128)S(1)}, ...), condition=%wide.region_8.9_spmd, body=%wide.region_2.8_spmd.sunk | while | flops 545257600 | bytes 8939898 | solution.py:144
  182.2 6.0 %conditional.2 = (f32[64,32]{0,1:T(8,128)S(1)}) conditional(s32[]{:T(128)} %convert_element_type.48, () %tuple.54, (s32[]{:T(128)}, bf16[128,64,2048]{2,1,0:T(8,128)(2,1)}, s32[]{:T(128)}, bf16[64,256,128]{0,1,2:T(8,128)(2,1)}) %tuple.55), branch_computations={%region_5.5_spmd, %region_6.7_spmd} | conditional | flops 545257472 | bytes 8922700 | solution.py:141
  182.2 6.0 %abs_reduce_fusion = f32[32,64]{1,0:T(8,128)S(1)} fusion(bf16[128,64,2048]{2,1,0:T(8,128)(2,1)} %get-tuple-element.172, s32[]{:T(128)S(6)} %select_n.87, bf16[64,256,128]{0,1,2:T(8,128)(2,1)} %get-tuple-element.174, s32[]{:T(128)S(6)} %select_n.88), kind=kOutput, calls=%fused_computation | convolution fusion | flops 545257472 | bytes 8922624 | tf_op jit(solution)/shard_map/while/body/eval_jaxpr/cond/branch_1_fun/hij,jhe->ije/dot_general | solution.py:133
  192.0 6.0 %conditional.2 = (f32[64,32]{0,1:T(8,128)S(1)}) conditional(s32[]{:T(128)} %convert_element_type.48, () %tuple.54, (s32[]{:T(128)}, bf16[128,64,2048]{2,1,0:T(8,128)(2,1)}, s32[]{:T(128)}, bf16[64,256,128]{0,1,2:T(8,128)(2,1)}) %tuple.55), branch_computations={%region_5.5_spmd, %region_6.7_spmd} | conditional | flops 545257472 | bytes 8922700 | solution.py:141
  192.0 6.0 %abs_reduce_fusion = f32[32,64]{1,0:T(8,128)S(1)} fusion(bf16[128,64,2048]{2,1,0:T(8,128)(2,1)} %get-tuple-element.172, s32[]{:T(128)S(6)} %select_n.87, bf16[64,256,128]{0,1,2:T(8,128)(2,1)} %get-tuple-element.174, s32[]{:T(128)S(6)} %select_n.88), kind=kOutput, calls=%fused_computation | convolution fusion | flops 545257472 | bytes 8922624 | tf_op jit(solution)/shard_map/while/body/eval_jaxpr/cond/branch_1_fun/hij,jhe->ije/dot_general | solution.py:133
  201.8 6.0 %conditional.2 = (f32[64,32]{0,1:T(8,128)S(1)}) conditional(s32[]{:T(128)} %convert_element_type.48, () %tuple.54, (s32[]{:T(128)}, bf16[128,64,2048]{2,1,0:T(8,128)(2,1)}, s32[]{:T(128)}, bf16[64,256,128]{0,1,2:T(8,128)(2,1)}) %tuple.55), branch_computations={%region_5.5_spmd, %region_6.7_spmd} | conditional | flops 545257472 | bytes 8922700 | solution.py:141
  201.8 6.0 %abs_reduce_fusion = f32[32,64]{1,0:T(8,128)S(1)} fusion(bf16[128,64,2048]{2,1,0:T(8,128)(2,1)} %get-tuple-element.172, s32[]{:T(128)S(6)} %select_n.87, bf16[64,256,128]{0,1,2:T(8,128)(2,1)} %get-tuple-element.174, s32[]{:T(128)S(6)} %select_n.88), kind=kOutput, calls=%fused_computation | convolution fusion | flops 545257472 | bytes 8922624 | tf_op jit(solution)/shard_map/while/body/eval_jaxpr/cond/branch_1_fun/hij,jhe->ije/dot_general | solution.py:133
  211.6 6.0 %conditional.2 = (f32[64,32]{0,1:T(8,128)S(1)}) conditional(s32[]{:T(128)} %convert_element_type.48, () %tuple.54, (s32[]{:T(128)}, bf16[128,64,2048]{2,1,0:T(8,128)(2,1)}, s32[]{:T(128)}, bf16[64,256,128]{0,1,2:T(8,128)(2,1)}) %tuple.55), branch_computations={%region_5.5_spmd, %region_6.7_spmd} | conditional | flops 545257472 | bytes 8922700 | solution.py:141
  211.6 6.0 %abs_reduce_fusion = f32[32,64]{1,0:T(8,128)S(1)} fusion(bf16[128,64,2048]{2,1,0:T(8,128)(2,1)} %get-tuple-element.172, s32[]{:T(128)S(6)} %select_n.87, bf16[64,256,128]{0,1,2:T(8,128)(2,1)} %get-tuple-element.174, s32[]{:T(128)S(6)} %select_n.88), kind=kOutput, calls=%fused_computation | convolution fusion | flops 545257472 | bytes 8922624 | tf_op jit(solution)/shard_map/while/body/eval_jaxpr/cond/branch_1_fun/hij,jhe->ije/dot_general | solution.py:133
  221.2 6.0 %conditional.2 = (f32[64,32]{0,1:T(8,128)S(1)}) conditional(s32[]{:T(128)} %convert_element_type.48, () %tuple.54, (s32[]{:T(128)}, bf16[128,64,2048]{2,1,0:T(8,128)(2,1)}, s32[]{:T(128)}, bf16[64,256,128]{0,1,2:T(8,128)(2,1)}) %tuple.55), branch_computations={%region_5.5_spmd, %region_6.7_spmd} | conditional | flops 545257472 | bytes 8922700 | solution.py:141
  221.2 6.0 %abs_reduce_fusion = f32[32,64]{1,0:T(8,128)S(1)} fusion(bf16[128,64,2048]{2,1,0:T(8,128)(2,1)} %get-tuple-element.172, s32[]{:T(128)S(6)} %select_n.87, bf16[64,256,128]{0,1,2:T(8,128)(2,1)} %get-tuple-element.174, s32[]{:T(128)S(6)} %select_n.88), kind=kOutput, calls=%fused_computation | convolution fusion | flops 545257472 | bytes 8922624 | tf_op jit(solution)/shard_map/while/body/eval_jaxpr/cond/branch_1_fun/hij,jhe->ije/dot_general | solution.py:133
  231.2 6.0 %conditional.2 = (f32[64,32]{0,1:T(8,128)S(1)}) conditional(s32[]{:T(128)} %convert_element_type.48, () %tuple.54, (s32[]{:T(128)}, bf16[128,64,2048]{2,1,0:T(8,128)(2,1)}, s32[]{:T(128)}, bf16[64,256,128]{0,1,2:T(8,128)(2,1)}) %tuple.55), branch_computations={%region_5.5_spmd, %region_6.7_spmd} | conditional | flops 545257472 | bytes 8922700 | solution.py:141
  231.3 6.0 %abs_reduce_fusion = f32[32,64]{1,0:T(8,128)S(1)} fusion(bf16[128,64,2048]{2,1,0:T(8,128)(2,1)} %get-tuple-element.172, s32[]{:T(128)S(6)} %select_n.87, bf16[64,256,128]{0,1,2:T(8,128)(2,1)} %get-tuple-element.174, s32[]{:T(128)S(6)} %select_n.88), kind=kOutput, calls=%fused_computation | convolution fusion | flops 545257472 | bytes 8922624 | tf_op jit(solution)/shard_map/while/body/eval_jaxpr/cond/branch_1_fun/hij,jhe->ije/dot_general | solution.py:133
  241.3 6.0 %conditional.2 = (f32[64,32]{0,1:T(8,128)S(1)}) conditional(s32[]{:T(128)} %convert_element_type.48, () %tuple.54, (s32[]{:T(128)}, bf16[128,64,2048]{2,1,0:T(8,128)(2,1)}, s32[]{:T(128)}, bf16[64,256,128]{0,1,2:T(8,128)(2,1)}) %tuple.55), branch_computations={%region_5.5_spmd, %region_6.7_spmd} | conditional | flops 545257472 | bytes 8922700 | solution.py:141
  241.3 6.0 %abs_reduce_fusion = f32[32,64]{1,0:T(8,128)S(1)} fusion(bf16[128,64,2048]{2,1,0:T(8,128)(2,1)} %get-tuple-element.172, s32[]{:T(128)S(6)} %select_n.87, bf16[64,256,128]{0,1,2:T(8,128)(2,1)} %get-tuple-element.174, s32[]{:T(128)S(6)} %select_n.88), kind=kOutput, calls=%fused_computation | convolution fusion | flops 545257472 | bytes 8922624 | tf_op jit(solution)/shard_map/while/body/eval_jaxpr/cond/branch_1_fun/hij,jhe->ije/dot_general | solution.py:133
  251.4 6.0 %conditional.2 = (f32[64,32]{0,1:T(8,128)S(1)}) conditional(s32[]{:T(128)} %convert_element_type.48, () %tuple.54, (s32[]{:T(128)}, bf16[128,64,2048]{2,1,0:T(8,128)(2,1)}, s32[]{:T(128)}, bf16[64,256,128]{0,1,2:T(8,128)(2,1)}) %tuple.55), branch_computations={%region_5.5_spmd, %region_6.7_spmd} | conditional | flops 545257472 | bytes 8922700 | solution.py:141
  251.4 6.0 %abs_reduce_fusion = f32[32,64]{1,0:T(8,128)S(1)} fusion(bf16[128,64,2048]{2,1,0:T(8,128)(2,1)} %get-tuple-element.172, s32[]{:T(128)S(6)} %select_n.87, bf16[64,256,128]{0,1,2:T(8,128)(2,1)} %get-tuple-element.174, s32[]{:T(128)S(6)} %select_n.88), kind=kOutput, calls=%fused_computation | convolution fusion | flops 545257472 | bytes 8922624 | tf_op jit(solution)/shard_map/while/body/eval_jaxpr/cond/branch_1_fun/hij,jhe->ije/dot_general | solution.py:133
  261.3 6.0 %conditional.2 = (f32[64,32]{0,1:T(8,128)S(1)}) conditional(s32[]{:T(128)} %convert_element_type.48, () %tuple.54, (s32[]{:T(128)}, bf16[128,64,2048]{2,1,0:T(8,128)(2,1)}, s32[]{:T(128)}, bf16[64,256,128]{0,1,2:T(8,128)(2,1)}) %tuple.55), branch_computations={%region_5.5_spmd, %region_6.7_spmd} | conditional | flops 545257472 | bytes 8922700 | solution.py:141
  261.3 6.0 %abs_reduce_fusion = f32[32,64]{1,0:T(8,128)S(1)} fusion(bf16[128,64,2048]{2,1,0:T(8,128)(2,1)} %get-tuple-element.172, s32[]{:T(128)S(6)} %select_n.87, bf16[64,256,128]{0,1,2:T(8,128)(2,1)} %get-tuple-element.174, s32[]{:T(128)S(6)} %select_n.88), kind=kOutput, calls=%fused_computation | convolution fusion | flops 545257472 | bytes 8922624 | tf_op jit(solution)/shard_map/while/body/eval_jaxpr/cond/branch_1_fun/hij,jhe->ije/dot_general | solution.py:133
  270.9 6.0 %conditional.2 = (f32[64,32]{0,1:T(8,128)S(1)}) conditional(s32[]{:T(128)} %convert_element_type.48, () %tuple.54, (s32[]{:T(128)}, bf16[128,64,2048]{2,1,0:T(8,128)(2,1)}, s32[]{:T(128)}, bf16[64,256,128]{0,1,2:T(8,128)(2,1)}) %tuple.55), branch_computations={%region_5.5_spmd, %region_6.7_spmd} | conditional | flops 545257472 | bytes 8922700 | solution.py:141
  270.9 6.0 %abs_reduce_fusion = f32[32,64]{1,0:T(8,128)S(1)} fusion(bf16[128,64,2048]{2,1,0:T(8,128)(2,1)} %get-tuple-element.172, s32[]{:T(128)S(6)} %select_n.87, bf16[64,256,128]{0,1,2:T(8,128)(2,1)} %get-tuple-element.174, s32[]{:T(128)S(6)} %select_n.88), kind=kOutput, calls=%fused_computation | convolution fusion | flops 545257472 | bytes 8922624 | tf_op jit(solution)/shard_map/while/body/eval_jaxpr/cond/branch_1_fun/hij,jhe->ije/dot_general | solution.py:133
  280.4 6.0 %conditional.2 = (f32[64,32]{0,1:T(8,128)S(1)}) conditional(s32[]{:T(128)} %convert_element_type.48, () %tuple.54, (s32[]{:T(128)}, bf16[128,64,2048]{2,1,0:T(8,128)(2,1)}, s32[]{:T(128)}, bf16[64,256,128]{0,1,2:T(8,128)(2,1)}) %tuple.55), branch_computations={%region_5.5_spmd, %region_6.7_spmd} | conditional | flops 545257472 | bytes 8922700 | solution.py:141
  280.5 6.0 %abs_reduce_fusion = f32[32,64]{1,0:T(8,128)S(1)} fusion(bf16[128,64,2048]{2,1,0:T(8,128)(2,1)} %get-tuple-element.172, s32[]{:T(128)S(6)} %select_n.87, bf16[64,256,128]{0,1,2:T(8,128)(2,1)} %get-tuple-element.174, s32[]{:T(128)S(6)} %select_n.88), kind=kOutput, calls=%fused_computation | convolution fusion | flops 545257472 | bytes 8922624 | tf_op jit(solution)/shard_map/while/body/eval_jaxpr/cond/branch_1_fun/hij,jhe->ije/dot_general | solution.py:133
  290.0 6.0 %conditional.2 = (f32[64,32]{0,1:T(8,128)S(1)}) conditional(s32[]{:T(128)} %convert_element_type.48, () %tuple.54, (s32[]{:T(128)}, bf16[128,64,2048]{2,1,0:T(8,128)(2,1)}, s32[]{:T(128)}, bf16[64,256,128]{0,1,2:T(8,128)(2,1)}) %tuple.55), branch_computations={%region_5.5_spmd, %region_6.7_spmd} | conditional | flops 545257472 | bytes 8922700 | solution.py:141
  290.1 6.0 %abs_reduce_fusion = f32[32,64]{1,0:T(8,128)S(1)} fusion(bf16[128,64,2048]{2,1,0:T(8,128)(2,1)} %get-tuple-element.172, s32[]{:T(128)S(6)} %select_n.87, bf16[64,256,128]{0,1,2:T(8,128)(2,1)} %get-tuple-element.174, s32[]{:T(128)S(6)} %select_n.88), kind=kOutput, calls=%fused_computation | convolution fusion | flops 545257472 | bytes 8922624 | tf_op jit(solution)/shard_map/while/body/eval_jaxpr/cond/branch_1_fun/hij,jhe->ije/dot_general | solution.py:133
  299.5 6.0 %conditional.2 = (f32[64,32]{0,1:T(8,128)S(1)}) conditional(s32[]{:T(128)} %convert_element_type.48, () %tuple.54, (s32[]{:T(128)}, bf16[128,64,2048]{2,1,0:T(8,128)(2,1)}, s32[]{:T(128)}, bf16[64,256,128]{0,1,2:T(8,128)(2,1)}) %tuple.55), branch_computations={%region_5.5_spmd, %region_6.7_spmd} | conditional | flops 545257472 | bytes 8922700 | solution.py:141
  299.5 6.0 %abs_reduce_fusion = f32[32,64]{1,0:T(8,128)S(1)} fusion(bf16[128,64,2048]{2,1,0:T(8,128)(2,1)} %get-tuple-element.172, s32[]{:T(128)S(6)} %select_n.87, bf16[64,256,128]{0,1,2:T(8,128)(2,1)} %get-tuple-element.174, s32[]{:T(128)S(6)} %select_n.88), kind=kOutput, calls=%fused_computation | convolution fusion | flops 545257472 | bytes 8922624 | tf_op jit(solution)/shard_map/while/body/eval_jaxpr/cond/branch_1_fun/hij,jhe->ije/dot_general | solution.py:133
  309.4 6.0 %conditional.2 = (f32[64,32]{0,1:T(8,128)S(1)}) conditional(s32[]{:T(128)} %convert_element_type.48, () %tuple.54, (s32[]{:T(128)}, bf16[128,64,2048]{2,1,0:T(8,128)(2,1)}, s32[]{:T(128)}, bf16[64,256,128]{0,1,2:T(8,128)(2,1)}) %tuple.55), branch_computations={%region_5.5_spmd, %region_6.7_spmd} | conditional | flops 545257472 | bytes 8922700 | solution.py:141
  309.4 6.0 %abs_reduce_fusion = f32[32,64]{1,0:T(8,128)S(1)} fusion(bf16[128,64,2048]{2,1,0:T(8,128)(2,1)} %get-tuple-element.172, s32[]{:T(128)S(6)} %select_n.87, bf16[64,256,128]{0,1,2:T(8,128)(2,1)} %get-tuple-element.174, s32[]{:T(128)S(6)} %select_n.88), kind=kOutput, calls=%fused_computation | convolution fusion | flops 545257472 | bytes 8922624 | tf_op jit(solution)/shard_map/while/body/eval_jaxpr/cond/branch_1_fun/hij,jhe->ije/dot_general | solution.py:133
  319.2 6.0 %conditional.2 = (f32[64,32]{0,1:T(8,128)S(1)}) conditional(s32[]{:T(128)} %convert_element_type.48, () %tuple.54, (s32[]{:T(128)}, bf16[128,64,2048]{2,1,0:T(8,128)(2,1)}, s32[]{:T(128)}, bf16[64,256,128]{0,1,2:T(8,128)(2,1)}) %tuple.55), branch_computations={%region_5.5_spmd, %region_6.7_spmd} | conditional | flops 545257472 | bytes 8922700 | solution.py:141
  319.2 6.0 %abs_reduce_fusion = f32[32,64]{1,0:T(8,128)S(1)} fusion(bf16[128,64,2048]{2,1,0:T(8,128)(2,1)} %get-tuple-element.172, s32[]{:T(128)S(6)} %select_n.87, bf16[64,256,128]{0,1,2:T(8,128)(2,1)} %get-tuple-element.174, s32[]{:T(128)S(6)} %select_n.88), kind=kOutput, calls=%fused_computation | convolution fusion | flops 545257472 | bytes 8922624 | tf_op jit(solution)/shard_map/while/body/eval_jaxpr/cond/branch_1_fun/hij,jhe->ije/dot_general | solution.py:133
  329.1 6.0 %conditional.2 = (f32[64,32]{0,1:T(8,128)S(1)}) conditional(s32[]{:T(128)} %convert_element_type.48, () %tuple.54, (s32[]{:T(128)}, bf16[128,64,2048]{2,1,0:T(8,128)(2,1)}, s32[]{:T(128)}, bf16[64,256,128]{0,1,2:T(8,128)(2,1)}) %tuple.55), branch_computations={%region_5.5_spmd, %region_6.7_spmd} | conditional | flops 545257472 | bytes 8922700 | solution.py:141
  329.1 6.0 %abs_reduce_fusion = f32[32,64]{1,0:T(8,128)S(1)} fusion(bf16[128,64,2048]{2,1,0:T(8,128)(2,1)} %get-tuple-element.172, s32[]{:T(128)S(6)} %select_n.87, bf16[64,256,128]{0,1,2:T(8,128)(2,1)} %get-tuple-element.174, s32[]{:T(128)S(6)} %select_n.88), kind=kOutput, calls=%fused_computation | convolution fusion | flops 545257472 | bytes 8922624 | tf_op jit(solution)/shard_map/while/body/eval_jaxpr/cond/branch_1_fun/hij,jhe->ije/dot_general | solution.py:133
  335.9 8.8 %all_to_all.16 = f32[4,256,32]{1,2,0:T(8,128)S(1)} all-to-all(f32[4,256,32]{1,2,0:T(8,128)S(1)} %bitcast.40), channel_id=1, replica_groups=mesh['width'=4,'row'=4,'src'=8] {'width'}, dimensions={0} | all-to-all | bytes 262144 | tf_op jit(solution)/shard_map/all_to_all | solution.py:55
  345.4 5.5 %all-to-all-start.2 = ((f32[32,1,256]{2,1,0:T(1,128)}), f32[32,1,256]{2,1,0:T(1,128)S(1)}, u32[]{:S(2)}, u32[]{:S(2)}) async-start(f32[32,1,256]{2,1,0:T(1,128)} %broadcast_in_dim.46), calls=%async_computation.2 | async-start | bytes 65536 | tf_op jit(solution)/shard_map/all_to_all | solution.py:14
  351.0 7.2 %all-to-all-done.2 = f32[32,1,256]{2,1,0:T(1,128)S(1)} async-done(((f32[32,1,256]{2,1,0:T(1,128)}), f32[32,1,256]{2,1,0:T(1,128)S(1)}, u32[]{:S(2)}, u32[]{:S(2)}) %all-to-all-start.2) | async-done | bytes 32800 | tf_op jit(solution)/shard_map/all_to_all | solution.py:14
  (90 shorter events, 58.0 us)
Async XLA Ops:
  6.5 2.2 copy-start.2
  6.5 118.6 %all-gather.2.cloned.1.call-start = ((), (), s32[]{:S(2)}) async-start(), calls=%async_computation.3 | async-start | bytes 34603008 | tf_op jit(solution)/shard_map/all_gather | solution.py:105
  9.5 6.5 %copy-start = (f32[2,128,256,8]{2,1,3,0:T(8,128)}, f32[2,128,256,8]{2,1,3,0:T(8,128)S(1)}, u32[]{:S(2)}) copy-start(f32[2,128,256,8]{2,1,3,0:T(8,128)S(1)} %get-tuple-element.232) | copy-start | bytes 6291460
  10.9 11.5 %all-to-all-start = ((f32[8,32,256]{2,1,0:T(8,128)}), f32[8,32,256]{2,1,0:T(8,128)S(1)}, u32[]{:S(2)}, u32[]{:S(2)}) async-start(f32[8,32,256]{2,1,0:T(8,128)} %broadcast_in_dim.44), calls=%async_computation | async-start | bytes 524288 | tf_op jit(solution)/shard_map/all_to_all | solution.py:14
  24.5 26.4 %collective-permute-start = (bf16[16,256,128]{2,1,0:T(8,128)(2,1)}, bf16[16,256,128]{2,1,0:T(8,128)(2,1)S(1)}, u32[]{:S(2)}, u32[]{:S(2)}) collective-permute-start(bf16[16,256,128]{2,1,0:T(8,128)(2,1)} %select_convert_fusion), channel_id=1, source_target_pairs={{0,32},{32,64},{64,96},{96,0},{1,33},{33,65},{65,97},{97,1},{2,34}... | collective-permute-start | bytes 3145736 | tf_op jit(solution)/shard_map/ppermute | solution.py:97
  51.0 24.3 %collective-permute-start.1 = (bf16[16,256,128]{2,1,0:T(8,128)(2,1)S(1)}, bf16[16,256,128]{2,1,0:T(8,128)(2,1)}, u32[]{:S(2)}, u32[]{:S(2)}) collective-permute-start(bf16[16,256,128]{2,1,0:T(8,128)(2,1)S(1)} %collective-permute-done), channel_id=1, source_target_pairs={{0,32},{32,64},{64,96},{96,0},{1,33},{33,65},{65,97},{97,1},{2,34}... | collective-permute-start | bytes 3145736 | tf_op jit(solution)/shard_map/ppermute | solution.py:97
  51.0 27.4 %collective-permute-start.2 = (bf16[16,256,128]{2,1,0:T(8,128)(2,1)}, bf16[16,256,128]{2,1,0:T(8,128)(2,1)}, u32[]{:S(2)}, u32[]{:S(2)}) collective-permute-start(bf16[16,256,128]{2,1,0:T(8,128)(2,1)} %select_convert_fusion), channel_id=1, source_target_pairs={{0,96},{32,0},{64,32},{96,64},{1,97},{33,1},{65,33},{97,65},{2,98}... | collective-permute-start | bytes 3145736 | tf_op jit(solution)/shard_map/ppermute | solution.py:99
  86.9 38.2 %copy-start.1 = (bf16[128,64,128]{2,1,0:T(8,128)(2,1)S(1)}, bf16[128,64,128]{2,1,0:T(8,128)(2,1)}, u32[]{:S(2)}) copy-start(bf16[128,64,128]{2,1,0:T(8,128)(2,1)} %convert_bitcast_fusion.1) | copy-start | bytes 6291460
  345.4 12.8 %all-to-all-start.2 = ((f32[32,1,256]{2,1,0:T(1,128)}), f32[32,1,256]{2,1,0:T(1,128)S(1)}, u32[]{:S(2)}, u32[]{:S(2)}) async-start(f32[32,1,256]{2,1,0:T(1,128)} %broadcast_in_dim.46), calls=%async_computation.2 | async-start | bytes 65536 | tf_op jit(solution)/shard_map/all_to_all | solution.py:14
Sparse Core Ops, SparseCore 0:
  9.6 115.4 all-gather.1
